TPU v7x, 32 devices: a whole 2x2x4 slice. The times are simulated.
32 devices in a mesh: row: 8 (over y, x, core), col: 4 (over z).
Axes of the slice: x: 2, y: 2, z: 4, core: 2. Of those that a mesh axis runs over, the one named last changes fastest.
Arguments:
- inputs_act: bfloat16 [1024, 4096], P('row', 'col'), may hold values from -6 to 6
- out_grad: bfloat16 [1024, 4096], P('row', 'col'), may hold values from -6 to 6
- pre_act: bfloat16 [1024, 16384], P('col', 'row'), may hold values from -8 to 8
- w_first: bfloat16 [4096, 16384], P('col', 'row'), may hold values from -0.046875 to 0.046875
- w_second: bfloat16 [16384, 4096], P('row', 'col'), may hold values from -0.09375 to 0.09375
Outputs:
- grad_input: bfloat16 [1024, 4096], P('row', 'col')
- grad_first: float32 [4096, 16384], P('col', 'row')
- grad_second: float32 [16384, 4096], P('row', 'col')
All inputs are finite; a program needn't handle non-finite values.
Results may differ from a plain program's by a relative error of at most 0.019.
Values may be sent and summed in bfloat16 or wider, within the bound.
A program may use at most 128 MiB of HBM per device.

v0:
```python
import math
import jax
import jax.numpy as jnp
from jax import lax
from jax.sharding import PartitionSpec as P

gelu_coef = 0.044715


def gelu_pair(pre_float):
    inner_c = math.sqrt(2.0 / math.pi)
    inner = inner_c * (pre_float + gelu_coef * pre_float * pre_float * pre_float)
    tanh_val = jnp.tanh(inner)
    act = 0.5 * pre_float * (1.0 + tanh_val)
    slope = 0.5 * (1.0 + tanh_val) + 0.5 * pre_float * (1.0 - tanh_val * tanh_val) * inner_c * (
        1.0 + 3.0 * gelu_coef * pre_float * pre_float
    )
    return (act, slope)


def contract_last(left, right):
    return lax.dot_general(
        left, right, (((1,), (1,)), ((), ())), preferred_element_type=jnp.float32
    )


def contract_first(left, right):
    return lax.dot_general(
        left, right, (((0,), (0,)), ((), ())), preferred_element_type=jnp.float32
    )


def on_device(inputs_act, out_grad, pre_act, w_first, w_second):
    total_tokens = pre_act.shape[0] * lax.axis_size("col")
    factor = 1.0 / math.sqrt(total_tokens)
    x_whole, dy_whole = (
        lax.all_gather(inputs_act, "row", axis=0, tiled=True),
        lax.all_gather(out_grad, "row", axis=0, tiled=True),
    )
    hidden_whole = lax.psum(contract_last(dy_whole, w_second).astype(jnp.bfloat16), "col").astype(
        jnp.float32
    )
    pre_whole = lax.all_gather(pre_act, "col", axis=0, tiled=True)
    act_float, slope = gelu_pair(pre_whole.astype(jnp.float32))
    act_whole = act_float.astype(jnp.bfloat16)
    grad_whole = (hidden_whole * slope).astype(jnp.bfloat16)
    grad_input = lax.psum_scatter(
        contract_last(grad_whole, w_first).astype(jnp.bfloat16),
        "row",
        scatter_dimension=0,
        tiled=True,
    )
    grad_first = contract_first(x_whole, grad_whole) * factor
    grad_second = contract_first(act_whole, dy_whole) * factor
    return (grad_input, grad_first, grad_second)


def solution(mesh):
    in_specs = (P("row", "col"), P("row", "col"), P("col", "row"), P("col", "row"), P("row", "col"))
    out_specs = (P("row", "col"), P("col", "row"), P("row", "col"))
    return jax.shard_map(
        on_device, mesh=mesh, in_specs=in_specs, out_specs=out_specs, check_vma=False
    )
```

profile of v0, /device:TPU:0, one launch (start us, length us, event | category | flops | bytes accessed | tf_op | source)
XLA Modules:
  0.0 360.1 jit_solution(10771306066762961557)
XLA Ops:
  7.2 0.0 all-gather.4.cloned.1.call-start
  7.2 0.7 all-gather.4.cloned.1.call-update
  7.9 0.0 all-gather.6.cloned.1.call-start
  7.9 0.7 all-gather.6.cloned.1.call-update
  8.6 0.0 all-reduce.2.cloned.1.call-start
  8.7 31.8 %all-gather.4.cloned.1.call-done = bf16[1024,1024]{1,0:T(8,128)(2,1)} async-done(((bf16[128,1024]{1,0:T(8,128)(2,1)}), bf16[1024,1024]{1,0:T(8,128)(2,1)}) %all-gather.4.cloned.1.call-update) | async-done | bytes 2097168 | tf_op jit(solution)/shard_map/all_gather | solution.py:38
  40.5 9.4 %convolution_convert_fusion = bf16[1024,2048]{1,0:T(8,128)(2,1)} fusion(bf16[1024,1024]{1,0:T(8,128)(2,1)} %all-gather.4.cloned.1.call-done, bf16[2048,1024]{1,0:T(8,128)(2,1)} %param.9), kind=kOutput, calls=%fused_computation.24 | convolution fusion | flops 4297064448 | bytes 10485760 | tf_op jit(solution)/shard_map/dot_general | solution.py:22
  49.9 0.0 all-reduce.2.cloned.1.call-update
  49.9 0.0 all-gather.8.cloned.1.call-start
  50.0 0.5 all-gather.8.cloned.1.call-update
  50.5 0.0 reduce-scatter.2.cloned.1.call-start
  50.5 72.3 %all-gather.6.cloned.1.call-done = bf16[1024,2048]{1,0:T(8,128)(2,1)} async-done(((bf16[256,2048]{1,0:T(8,128)(2,1)}), bf16[1024,2048]{1,0:T(8,128)(2,1)}) %all-gather.6.cloned.1.call-update) | async-done | bytes 4194320 | tf_op jit(solution)/shard_map/all_gather | solution.py:43
  122.9 156.5 %all-reduce.2.cloned.1.call-done = bf16[1024,2048]{1,0:T(8,128)(2,1)} async-done(((bf16[1024,2048]{1,0:T(8,128)(2,1)}), bf16[1024,2048]{1,0:T(8,128)(2,1)}) %all-reduce.2.cloned.1.call-update) | async-done | bytes 4194320 | tf_op jit(solution)/shard_map/psum | solution.py:40
  279.4 0.0 copy-start.1
  279.4 8.2 %fusion.6 = bf16[1024,2048]{1,0:T(8,128)(2,1)S(1)} fusion(bf16[1024,2048]{1,0:T(8,128)(2,1)} %all-gather.6.cloned.1.call-done, bf16[1024,2048]{1,0:T(8,128)(2,1)} %all-reduce.2.cloned.1.call-done), kind=kLoop, calls=%fused_computation.13 | loop fusion | flops 44040192 | bytes 12582912 | tf_op jit(solution)/shard_map/convert_element_type | solution.py:46
  287.6 0.0 copy-start
  287.6 2.0 copy-done
  289.6 0.0 copy-done.1
  289.6 0.0 copy-start.2
  289.6 5.7 %convolution_convert_fusion.1 = bf16[1024,1024]{1,0:T(8,128)(2,1)} fusion(bf16[1024,2048]{1,0:T(8,128)(2,1)S(1)} %fusion.6, bf16[1024,2048]{1,0:T(8,128)(2,1)S(1)} %copy-done.1), kind=kOutput, calls=%fused_computation.25 | convolution fusion | flops 4296015872 | bytes 10485760 | tf_op jit(solution)/shard_map/dot_general | solution.py:22
  295.4 0.0 reduce-scatter.2.cloned.1.call-update
  295.4 0.0 copy-done.2
  295.4 12.1 %convolution_multiply_fusion = f32[2048,1024]{1,0:T(8,128)} fusion(bf16[1024,1024]{1,0:T(8,128)(2,1)S(1)} %copy-done.2, bf16[1024,2048]{1,0:T(8,128)(2,1)} %all-gather.6.cloned.1.call-done), kind=kOutput, calls=%fused_computation.19 | convolution fusion | flops 4318035968 | bytes 14680064 | tf_op jit(solution)/shard_map/dot_general | solution.py:28
  307.5 0.7 all-gather.8.cloned.1.call-done
  308.2 10.6 %multiply_bitcast_fusion = f32[1024,2048]{0,1:T(8,128)} fusion(bf16[1024,2048]{1,0:T(8,128)(2,1)} %copy-done, bf16[1024,1024]{1,0:T(8,128)(2,1)} %all-gather.8.cloned.1.call-done), kind=kOutput, calls=%fused_computation.18 | convolution fusion | flops 4297064448 | bytes 14680064 | tf_op jit(solution)/shard_map/dot_general | solution.py:28
  318.9 9.3 %copy.8 = f32[1024,2048]{1,0:T(8,128)} copy(f32[1024,2048]{0,1:T(8,128)} %multiply_bitcast_fusion) | data formatting | bytes 16777216
  328.2 25.3 %reduce-scatter.2.cloned.1.call-done = bf16[128,1024]{1,0:T(8,128)(2,1)} async-done(((bf16[1024,1024]{1,0:T(8,128)(2,1)}), bf16[128,1024]{1,0:T(8,128)(2,1)}) %reduce-scatter.2.cloned.1.call-update) | async-done | bytes 262160 | tf_op jit(solution)/shard_map/reduce_scatter | solution.py:47
Async XLA Ops:
  7.2 33.4 %all-gather.4.cloned.1.call-start = ((), (), s32[]{:S(2)}) async-start(), calls=%async_computation.1 | async-start | bytes 2359296 | tf_op jit(solution)/shard_map/all_gather | solution.py:38
  7.9 115.0 %all-gather.6.cloned.1.call-start = ((), (), s32[]{:S(2)}) async-start(), calls=%async_computation.3 | async-start | bytes 5242880 | tf_op jit(solution)/shard_map/all_gather | solution.py:43
  8.6 270.7 %all-reduce.2.cloned.1.call-start = ((), (), s32[]{:S(2)}) async-start(), calls=%async_computation.2 | async-start | bytes 8388608 | tf_op jit(solution)/shard_map/psum | solution.py:40
  49.9 258.3 %all-gather.8.cloned.1.call-start = ((), (), s32[]{:S(2)}) async-start(), calls=%async_computation.5 | async-start | bytes 2359296 | tf_op jit(solution)/shard_map/all_gather | solution.py:37
  50.5 303.0 %reduce-scatter.2.cloned.1.call-start = ((), (), s32[]{:S(2)}) async-start(), calls=%async_computation.4 | async-start | bytes 2359296 | tf_op jit(solution)/shard_map/reduce_scatter | solution.py:47
  279.4 10.3 %copy-start.1 = (bf16[1024,2048]{1,0:T(8,128)(2,1)S(1)}, bf16[1024,2048]{1,0:T(8,128)(2,1)}, u32[]{:S(2)}) copy-start(bf16[1024,2048]{1,0:T(8,128)(2,1)} %param.8) | copy-start | bytes 12582916
  287.6 2.0 copy-start
  289.6 5.8 %copy-start.2 = (bf16[1024,1024]{1,0:T(8,128)(2,1)S(1)}, bf16[1024,1024]{1,0:T(8,128)(2,1)}, u32[]{:S(2)}) copy-start(bf16[1024,1024]{1,0:T(8,128)(2,1)} %all-gather.4.cloned.1.call-done) | copy-start | bytes 6291460
Sparse Core Ops, SparseCore 0:
  9.9 30.5 all-gather.3
  42.1 80.7 all-gather.5
  125.8 153.4 all-reduce.1
  281.3 26.8 all-gather.7
  312.3 41.2 reduce-scatter.1
where the time goes:
time: 360 us
  waiting for transfers between devices  289 us (80%)
  matrix products  37.8 us (10%)
  between operations  13.8 us (4%)
  local copies, waits for them, and re-layouts  11.3 us (3%)
  other arithmetic  8.23 us (2%)
    psum x1, waiting for transfers between devices, on_device(): lax.psum(contract_last(dy_whole, w_second).astype(jnp.bfloat16), 'col')  156 us
    all_gather x1, waiting for transfers between devices, on_device(): pre_whole = lax.all_gather(pre_act, 'col', axis=0, tiled=True)  72.3 us
    all_gather x1, waiting for transfers between devices, on_device(): lax.all_gather(out_grad, 'row', axis=0, tiled=True)  31.8 us
    reduce_scatter x1, waiting for transfers between devices, on_device(): lax.psum_scatter(contract_last(grad_whole, w_first).astype(jnp.bfloat16),...  25.3 us
    dot_general x2, matrix products, contract_first(): lax.dot_general(left, right, (((0,), (0,)), ((), ())), preferred_element_...  22.7 us
    dot_general x2, matrix products, contract_last(): lax.dot_general(left, right, (((1,), (1,)), ((), ())), preferred_element_...  15.1 us
    unnamed x7, local copies, waits for them, and re-layouts  11.3 us
    convert_element_type x1, other arithmetic, on_device(): grad_whole = (hidden_whole * slope).astype(jnp.bfloat16)  8.23 us
  transfers between devices with their start and end apart: 5, of which 5 were waited for; matrix products, arithmetic and copies ran while one was open for 15% of the time, Pallas kernels for 0%

commit v1 on v0

--- a/solution.py
+++ b/solution.py
@@ -5,6 +5,22 @@
 from jax.sharding import PartitionSpec as P
 
 gelu_coef = 0.044715
+
+
+def ring_gather(x, axis, dim):
+    ways, here, lap = (lax.axis_size(axis), lax.axis_index(axis), x.shape[dim])
+    dims = [n * ways if d == dim else n for d, n in enumerate(x.shape)]
+    full = lax.dynamic_update_slice_in_dim(jnp.zeros(dims, x.dtype), x, here * lap, axis=dim)
+    going_up = going_down = x
+    for far in range(1, ways // 2 + 1):
+        going_up = lax.ppermute(going_up, axis, [(d, (d + 1) % ways) for d in range(ways)])
+        full = lax.dynamic_update_slice_in_dim(full, going_up, (here - far) % ways * lap, axis=dim)
+        if 2 * far < ways:
+            going_down = lax.ppermute(going_down, axis, [(d, (d - 1) % ways) for d in range(ways)])
+            full = lax.dynamic_update_slice_in_dim(
+                full, going_down, (here + far) % ways * lap, axis=dim
+            )
+    return full
 
 
 def gelu_pair(pre_float):
@@ -40,7 +56,7 @@
     hidden_whole = lax.psum(contract_last(dy_whole, w_second).astype(jnp.bfloat16), "col").astype(
         jnp.float32
     )
-    pre_whole = lax.all_gather(pre_act, "col", axis=0, tiled=True)
+    pre_whole = ring_gather(pre_act, "col", 0)
     act_float, slope = gelu_pair(pre_whole.astype(jnp.float32))
     act_whole = act_float.astype(jnp.bfloat16)
     grad_whole = (hidden_whole * slope).astype(jnp.bfloat16)

time: 360 us -> 349 us (0.969)
  waiting for transfers between devices: 289 us -> 221 us
  starting transfers between devices: 0.19 us -> 47.2 us
  local copies, waits for them, and re-layouts: 11.3 us -> 20.5 us
    ppermute x0 -> x3, waiting for transfers between devices: none -> 82.3 us  [the longest x2 82.3 us: ring_gather(): lax.ppermute(going_up, axis, [(d, (d + 1) % ways) for d in range(ways)])]
    psum x1, waiting for transfers between devices: 156 us -> 78.8 us  [on_device(): lax.psum(contract_last(dy_whole, w_second).astype(jnp.bfloat16), 'col')]
    all_gather x1 -> x0, waiting for transfers between devices: 72.3 us -> none  [on_device(): pre_whole = lax.all_gather(pre_act, 'col', axis=0, tiled=True)]
    ppermute x0 -> x3, starting transfers between devices: none -> 47.1 us  [the longest x2 44.7 us: ring_gather(): lax.ppermute(going_up, axis, [(d, (d + 1) % ways) for d in range(ways)])]
    dynamic_update_slice x0 -> x4, local copies, waits for them, and re-layouts: none -> 5.54 us  [the longest x1 2.3 us: ring_gather(): lax.dynamic_update_slice_in_dim(full, going_down, (here + far) % ways * l...]
    unnamed x7 -> x9, local copies, waits for them, and re-layouts: 11.3 us -> 12.5 us
  transfers between devices with their start and end apart: 5 -> 7, of which waited for: 5 -> 6; matrix products, arithmetic and copies ran while one was open for 15% -> 16% of each run, Pallas kernels for 0% -> 0%
where the time goes in v1:
time: 349 us; the launch traced here: 348 us
  waiting for transfers between devices  221 us (63%)
  starting transfers between devices  47.2 us (14%)
  matrix products  37.8 us (11%)
  local copies, waits for them, and re-layouts  20.5 us (6%)
  between operations  13.9 us (4%)
  other arithmetic  8.23 us (2%)
    ppermute x2, waiting for transfers between devices, ring_gather(): lax.ppermute(going_up, axis, [(d, (d + 1) % ways) for d in range(ways)])  82.3 us
    psum x1, waiting for transfers between devices, on_device(): lax.psum(contract_last(dy_whole, w_second).astype(jnp.bfloat16), 'col')  78.8 us
    ppermute x2, starting transfers between devices, ring_gather(): lax.ppermute(going_up, axis, [(d, (d + 1) % ways) for d in range(ways)])  44.7 us
    all_gather x1, waiting for transfers between devices, on_device(): lax.all_gather(out_grad, 'row', axis=0, tiled=True)  32.6 us
    reduce_scatter x1, waiting for transfers between devices, on_device(): lax.psum_scatter(contract_last(grad_whole, w_first).astype(jnp.bfloat16),...  25.3 us
    dot_general x2, matrix products, contract_first(): lax.dot_general(left, right, (((0,), (0,)), ((), ())), preferred_element_...  22.7 us
    dot_general x2, matrix products, contract_last(): lax.dot_general(left, right, (((1,), (1,)), ((), ())), preferred_element_...  15.1 us
    unnamed x9, local copies, waits for them, and re-layouts  12.5 us
  transfers between devices with their start and end apart: 7, of which 6 were waited for; matrix products, arithmetic and copies ran while one was open for 16% of the time, Pallas kernels for 0%

profile of v1, /device:TPU:0, one launch (start us, length us, event | category | flops | bytes accessed | tf_op | source)
XLA Modules:
  0.0 348.4 jit_solution(12650305028992453630)
XLA Ops:
  7.2 0.0 all-gather.3.cloned.1.call-start
  7.2 0.7 all-gather.3.cloned.1.call-update
  7.9 0.0 all-reduce.2.cloned.1.call-start
  7.9 32.6 %all-gather.3.cloned.1.call-done = bf16[1024,1024]{1,0:T(8,128)(2,1)} async-done(((bf16[128,1024]{1,0:T(8,128)(2,1)}), bf16[1024,1024]{1,0:T(8,128)(2,1)}) %all-gather.3.cloned.1.call-update) | async-done | bytes 2097168 | tf_op jit(solution)/shard_map/all_gather | solution.py:54
  40.5 9.4 %convolution_convert_fusion = bf16[1024,2048]{1,0:T(8,128)(2,1)} fusion(bf16[1024,1024]{1,0:T(8,128)(2,1)} %all-gather.3.cloned.1.call-done, bf16[2048,1024]{1,0:T(8,128)(2,1)} %param.9), kind=kOutput, calls=%fused_computation.24 | convolution fusion | flops 4297064448 | bytes 10485760 | tf_op jit(solution)/shard_map/dot_general | solution.py:38
  49.9 0.0 all-reduce.2.cloned.1.call-update
  49.9 0.0 all-gather.5.cloned.1.call-start
  50.0 1.1 copy-done.1
  51.1 1.5 collective-permute-start
  52.6 2.3 collective-permute-start.1
  54.9 43.5 %collective-permute-done = bf16[256,2048]{1,0:T(8,128)(2,1)S(1)} collective-permute-done((bf16[256,2048]{1,0:T(8,128)(2,1)S(1)}, bf16[256,2048]{1,0:T(8,128)(2,1)S(1)}, u32[]{:S(2)}, u32[]{:S(2)}) %collective-permute-start) | collective-permute-done | bytes 1048608 | tf_op jit(solution)/shard_map/ppermute | solution.py:16
  98.4 43.2 %collective-permute-start.2 = (bf16[256,2048]{1,0:T(8,128)(2,1)S(1)}, bf16[256,2048]{1,0:T(8,128)(2,1)S(1)}, u32[]{:S(2)}, u32[]{:S(2)}) collective-permute-start(bf16[256,2048]{1,0:T(8,128)(2,1)S(1)} %collective-permute-done), channel_id=1, source_target_pairs={{0,1},{1,2},{2,3},{3,0},{4,5},{5,6},{6,7},{7,4},{8,9},{9,10},{10,1... | collective-permute-start | bytes 3145736 | tf_op jit(solution)/shard_map/ppermute | solution.py:16
  141.7 0.0 all-gather.5.cloned.1.call-update
  141.7 0.0 reduce-scatter.2.cloned.1.call-start
  141.8 2.5 broadcast_in_dim.3
  144.4 1.1 constant_dynamic-update-slice_fusion.3
  145.4 1.1 constant_dynamic-update-slice_fusion.2
  146.5 0.0 collective-permute-done.1
  146.5 2.3 constant_dynamic-update-slice_fusion.1
  148.9 38.8 %collective-permute-done.2 = bf16[256,2048]{1,0:T(8,128)(2,1)S(1)} collective-permute-done((bf16[256,2048]{1,0:T(8,128)(2,1)S(1)}, bf16[256,2048]{1,0:T(8,128)(2,1)S(1)}, u32[]{:S(2)}, u32[]{:S(2)}) %collective-permute-start.2) | collective-permute-done | bytes 1048608 | tf_op jit(solution)/shard_map/ppermute | solution.py:16
  187.7 1.1 constant_dynamic-update-slice_fusion
  188.7 78.8 %all-reduce.2.cloned.1.call-done = bf16[1024,2048]{1,0:T(8,128)(2,1)} async-done(((bf16[1024,2048]{1,0:T(8,128)(2,1)}), bf16[1024,2048]{1,0:T(8,128)(2,1)}) %all-reduce.2.cloned.1.call-update) | async-done | bytes 4194320 | tf_op jit(solution)/shard_map/psum | solution.py:56
  267.5 8.2 %fusion.6 = bf16[1024,2048]{1,0:T(8,128)(2,1)S(1)} fusion(bf16[1024,2048]{1,0:T(8,128)(2,1)} %constant_dynamic-update-slice_fusion, bf16[1024,2048]{1,0:T(8,128)(2,1)} %all-reduce.2.cloned.1.call-done), kind=kLoop, calls=%fused_computation.13 | loop fusion | flops 44040192 | bytes 12582912 | tf_op jit(solution)/shard_map/convert_element_type | solution.py:62
  275.8 2.0 copy-done
  277.7 5.8 %convolution_convert_fusion.1 = bf16[1024,1024]{1,0:T(8,128)(2,1)} fusion(bf16[1024,2048]{1,0:T(8,128)(2,1)S(1)} %fusion.6, bf16[1024,2048]{1,0:T(8,128)(2,1)S(1)} %copy-done.2), kind=kOutput, calls=%fused_computation.25 | convolution fusion | flops 4296015872 | bytes 10485760 | tf_op jit(solution)/shard_map/dot_general | solution.py:38
  283.5 0.0 reduce-scatter.2.cloned.1.call-update
  283.5 0.0 copy-done.3
  283.5 12.1 %convolution_multiply_fusion = f32[2048,1024]{1,0:T(8,128)} fusion(bf16[1024,1024]{1,0:T(8,128)(2,1)S(1)} %copy-done.3, bf16[1024,2048]{1,0:T(8,128)(2,1)} %constant_dynamic-update-slice_fusion), kind=kOutput, calls=%fused_computation.19 | convolution fusion | flops 4318035968 | bytes 14680064 | tf_op jit(solution)/shard_map/dot_general | solution.py:44
  295.6 0.9 all-gather.5.cloned.1.call-done
  296.5 10.7 %multiply_bitcast_fusion = f32[1024,2048]{0,1:T(8,128)} fusion(bf16[1024,2048]{1,0:T(8,128)(2,1)} %copy-done, bf16[1024,1024]{1,0:T(8,128)(2,1)} %all-gather.5.cloned.1.call-done), kind=kOutput, calls=%fused_computation.18 | convolution fusion | flops 4297064448 | bytes 14680064 | tf_op jit(solution)/shard_map/dot_general | solution.py:44
  307.2 9.3 %copy.8 = f32[1024,2048]{1,0:T(8,128)} copy(f32[1024,2048]{0,1:T(8,128)} %multiply_bitcast_fusion) | data formatting | bytes 16777216
  316.5 25.3 %reduce-scatter.2.cloned.1.call-done = bf16[128,1024]{1,0:T(8,128)(2,1)} async-done(((bf16[1024,1024]{1,0:T(8,128)(2,1)}), bf16[128,1024]{1,0:T(8,128)(2,1)}) %reduce-scatter.2.cloned.1.call-update) | async-done | bytes 262160 | tf_op jit(solution)/shard_map/reduce_scatter | solution.py:63
  (5 shorter events, 0.0 us)
Async XLA Ops:
  7.2 33.4 %all-gather.3.cloned.1.call-start = ((), (), s32[]{:S(2)}) async-start(), calls=%async_computation.1 | async-start | bytes 2359296 | tf_op jit(solution)/shard_map/all_gather | solution.py:54
  7.9 259.6 %all-reduce.2.cloned.1.call-start = ((), (), s32[]{:S(2)}) async-start(), calls=%async_computation.2 | async-start | bytes 8388608 | tf_op jit(solution)/shard_map/psum | solution.py:56
  49.9 1.2 copy-start.1
  49.9 246.6 %all-gather.5.cloned.1.call-start = ((), (), s32[]{:S(2)}) async-start(), calls=%async_computation.4 | async-start | bytes 2359296 | tf_op jit(solution)/shard_map/all_gather | solution.py:53
  51.1 47.3 %collective-permute-start = (bf16[256,2048]{1,0:T(8,128)(2,1)S(1)}, bf16[256,2048]{1,0:T(8,128)(2,1)S(1)}, u32[]{:S(2)}, u32[]{:S(2)}) collective-permute-start(bf16[256,2048]{1,0:T(8,128)(2,1)S(1)} %copy-done.1), channel_id=1, source_target_pairs={{0,1},{1,2},{2,3},{3,0},{4,5},{5,6},{6,7},{7,4},{8,9},{9,10},{10,1... | collective-permute-start | bytes 3145736 | tf_op jit(solution)/shard_map/ppermute | solution.py:16
  52.6 94.0 %collective-permute-start.1 = (bf16[256,2048]{1,0:T(8,128)(2,1)S(1)}, bf16[256,2048]{1,0:T(8,128)(2,1)}, u32[]{:S(2)}, u32[]{:S(2)}) collective-permute-start(bf16[256,2048]{1,0:T(8,128)(2,1)S(1)} %copy-done.1), channel_id=1, source_target_pairs={{0,3},{1,0},{2,1},{3,2},{4,7},{5,4},{6,5},{7,6},{8,11},{9,8},{10,9... | collective-permute-start | bytes 3145736 | tf_op jit(solution)/shard_map/ppermute | solution.py:19
  98.4 89.2 %collective-permute-start.2 = (bf16[256,2048]{1,0:T(8,128)(2,1)S(1)}, bf16[256,2048]{1,0:T(8,128)(2,1)S(1)}, u32[]{:S(2)}, u32[]{:S(2)}) collective-permute-start(bf16[256,2048]{1,0:T(8,128)(2,1)S(1)} %collective-permute-done), channel_id=1, source_target_pairs={{0,1},{1,2},{2,3},{3,0},{4,5},{5,6},{6,7},{7,4},{8,9},{9,10},{10,1... | collective-permute-start | bytes 3145736 | tf_op jit(solution)/shard_map/ppermute | solution.py:16
  141.7 200.1 %reduce-scatter.2.cloned.1.call-start = ((), (), s32[]{:S(2)}) async-start(), calls=%async_computation.3 | async-start | bytes 2359296 | tf_op jit(solution)/shard_map/reduce_scatter | solution.py:63
  267.5 10.2 %copy-start.2 = (bf16[1024,2048]{1,0:T(8,128)(2,1)S(1)}, bf16[1024,2048]{1,0:T(8,128)(2,1)}, u32[]{:S(2)}) copy-start(bf16[1024,2048]{1,0:T(8,128)(2,1)} %param.8) | copy-start | bytes 12582916
  275.8 2.0 copy-start
  277.7 5.8 %copy-start.3 = (bf16[1024,1024]{1,0:T(8,128)(2,1)S(1)}, bf16[1024,1024]{1,0:T(8,128)(2,1)}, u32[]{:S(2)}) copy-start(bf16[1024,1024]{1,0:T(8,128)(2,1)} %all-gather.3.cloned.1.call-done) | copy-start | bytes 6291460
Sparse Core Ops, SparseCore 0:
  9.9 30.5 all-gather.2
  50.0 217.4 all-reduce.1
  269.6 26.8 all-gather.4
  300.6 41.2 reduce-scatter.1
